TPU v7x, 512 devices: a whole 4x8x8 slice. The times are simulated.
512 devices in a mesh: dom: 16 (over z_lo, x, core), band: 32 (over z_hi, y).
Axes of the slice: x: 4, y: 8, z: 8 (z_hi: 4, z_lo: 2; z = z_hi * 2 + z_lo), core: 2. Of those that a mesh axis runs over, the one named last changes fastest.
Arguments:
- orbitals: bfloat16 [1024, 16, 2, 16, 128], P('band', 'dom'), may hold values from -6 to 6
- potential: float32 [16, 2, 16, 128], P('dom'), may hold values from -1 to 1
- ritz: bfloat16 [1024, 1024], P(None, 'band'), may hold values from -0.1875 to 0.1875
Outputs:
- rotated: float32 [1024, 16, 2, 16, 128], P('band', 'dom')
All inputs are finite; a program needn't handle non-finite values.
Results may differ from a plain program's by a relative error of at most 0.0029.
Values may be sent and summed in bfloat16 or wider, within the bound.
No kernel may reach another device: no remote copies, remote signals or barrier semaphores. Data moves between devices by JAX's collectives and lax.ppermute only.
A program may use at most 64 MiB of HBM per device.

v0:
```python
import math
import jax
import jax.numpy as jnp
from jax import lax
from jax.sharding import PartitionSpec as P

DEG = 4
lower_bound = -1.5
cut_off = 1.0
upper_bound = 9.5
coef_zero = -2.5
coef_one = 4.0 / 3.0
coef_two = -1.0 / 12.0


def shifted(value, axis, steps):
    count = lax.axis_size(axis)
    pairs = [(source, (source + steps) % count) for source in range(count)]
    return lax.ppermute(value, axis, pairs)


def filter_weights(degree):
    half_width = (upper_bound - cut_off) / 2.0
    centre = (upper_bound + cut_off) / 2.0
    sigma_now = half_width / (lower_bound - centre)
    first_scale = sigma_now / half_width
    inverse_gain = 2.0 / sigma_now
    weights = []
    for degree_step in range(1, degree):
        sigma_next = 1.0 / (inverse_gain - sigma_now)
        weights.append((2.0 * sigma_next / half_width, sigma_now * sigma_next))
        sigma_now = sigma_next
    return (centre, first_scale, weights)


def send_first(face, offset):
    return shifted(face, "dom", offset)


def send_second(face, offset):
    return shifted(face, "dom", offset)


def padded_second(padded, count, axis):
    lower_near = lax.slice_in_dim(padded, 1, count + 1, axis=axis)
    upper_near = lax.slice_in_dim(padded, 3, count + 3, axis=axis)
    lower_far = lax.slice_in_dim(padded, 0, count, axis=axis)
    upper_far = lax.slice_in_dim(padded, 4, count + 4, axis=axis)
    return coef_one * (lower_near + upper_near) + coef_two * (lower_far + upper_far)


def apply_ham(field_now, local_pot, grid_side, row_y):
    cells_x = field_now.shape[1]
    cells_y = field_now.shape[2]
    low_x = send_first(field_now, grid_side)
    high_x = send_first(field_now, -grid_side)
    along_x = jnp.concatenate([low_x, field_now, high_x], axis=1)
    top_y = field_now[:, :, cells_y - 2 :]
    bottom_y = field_now[:, :, :2]
    low_y = jnp.where(row_y == 0, send_second(top_y, 1 - grid_side), send_second(top_y, 1))
    high_y = jnp.where(
        row_y == grid_side - 1, send_second(bottom_y, grid_side - 1), send_second(bottom_y, -1)
    )
    along_y = jnp.concatenate([low_y, field_now, high_y], axis=2)
    near_z = jnp.roll(field_now, 1, 3) + jnp.roll(field_now, -1, 3)
    far_z = jnp.roll(field_now, 2, 3) + jnp.roll(field_now, -2, 3)
    second = (
        3.0 * coef_zero * field_now
        + padded_second(along_x, cells_x, 1)
        + padded_second(along_y, cells_y, 2)
    )
    second = second + (coef_one * near_z + coef_two * far_z)
    return -0.5 * second + local_pot * field_now


def on_device(orbitals, potential, ritz):
    grid_side = math.isqrt(lax.axis_size("dom"))
    row_y = lax.axis_index("dom") % grid_side
    centre, first_scale, weights = filter_weights(DEG)
    local_pot = potential[0]
    previous = orbitals[:, 0].astype(jnp.float32)
    current = (apply_ham(previous, local_pot, grid_side, row_y) - centre * previous) * first_scale
    for scale_h, scale_x in weights:
        following = (
            apply_ham(current, local_pot, grid_side, row_y) - centre * current
        ) * scale_h - scale_x * previous
        previous, current = (current, following)
    band_rows = current.shape[0]
    flat_panel = current.astype(jnp.bfloat16).reshape(band_rows, -1)
    rotated = lax.dot_general(
        ritz,
        lax.all_gather(flat_panel, "band", axis=0, tiled=True),
        (((0,), (0,)), ((), ())),
        preferred_element_type=jnp.float32,
    )
    return rotated.reshape(orbitals.shape)


def solution(mesh):
    in_specs = (P("band", "dom", None, None, None), P("dom", None, None, None), P(None, "band"))
    out_specs = P("band", "dom", None, None, None)
    return jax.shard_map(
        on_device, mesh=mesh, in_specs=in_specs, out_specs=out_specs, check_vma=False
    )
```

profile of v0, /device:TPU:1, one launch (start us, length us, event | category | flops | bytes accessed | tf_op | source)
XLA Modules:
  0.0 319.9 jit_solution(1605391283668732699)
XLA Ops:
  6.5 1.1 bitcast_convert_fusion
  7.6 0.7 fusion.99
  8.3 4.5 %collective-permute-start.3 = (f32[32,2,2,128]{3,2,1,0:T(2,128)}, f32[32,2,2,128]{3,2,1,0:T(2,128)}, u32[]{:S(2)}, u32[]{:S(2)}) collective-permute-start(f32[32,2,2,128]{3,2,1,0:T(2,128)} %get-tuple-element.37), channel_id=1, source_target_pairs={{0,32},{32,64},{64,96},{96,128},{128,160},{160,192},{192,224},{224... | collective-permute-start | bytes 196616 | tf_op jit(solution)/shard_map/ppermute | solution.py:19
  12.8 5.0 %collective-permute-start.2 = (f32[32,2,2,128]{3,2,1,0:T(2,128)}, f32[32,2,2,128]{3,2,1,0:T(2,128)}, u32[]{:S(2)}, u32[]{:S(2)}) collective-permute-start(f32[32,2,2,128]{3,2,1,0:T(2,128)} %get-tuple-element.37), channel_id=1, source_target_pairs={{0,416},{32,448},{64,480},{96,0},{128,32},{160,64},{192,96},{224,1... | collective-permute-start | bytes 196616 | tf_op jit(solution)/shard_map/ppermute | solution.py:19
  17.8 3.1 collective-permute-start.1
  20.9 3.7 %collective-permute-start = (f32[32,2,16,128]{3,2,1,0:T(8,128)S(1)}, f32[32,2,16,128]{3,2,1,0:T(8,128)}, u32[]{:S(2)}, u32[]{:S(2)}) collective-permute-start(f32[32,2,16,128]{3,2,1,0:T(8,128)S(1)} %bitcast_convert_fusion), channel_id=1, source_target_pairs={{0,128},{32,160},{64,192},{96,224},{128,256},{160,288},{192,320},{... | collective-permute-start | bytes 1572872 | tf_op jit(solution)/shard_map/ppermute | solution.py:19
  24.6 4.0 %collective-permute-start.5 = (f32[32,2,2,128]{3,2,1,0:T(2,128)}, f32[32,2,2,128]{3,2,1,0:T(2,128)}, u32[]{:S(2)}, u32[]{:S(2)}) collective-permute-start(f32[32,2,2,128]{3,2,1,0:T(2,128)} %get-tuple-element.38), channel_id=1, source_target_pairs={{0,480},{32,0},{64,32},{96,64},{128,96},{160,128},{192,160},{224,1... | collective-permute-start | bytes 196616 | tf_op jit(solution)/shard_map/ppermute | solution.py:19
  28.9 0.2 fusion.100
  29.1 1.0 fusion.103
  30.1 1.1 fusion.102
  31.3 4.4 %collective-permute-start.4 = (f32[32,2,2,128]{3,2,1,0:T(2,128)}, f32[32,2,2,128]{3,2,1,0:T(2,128)S(1)}, u32[]{:S(2)}, u32[]{:S(2)}) collective-permute-start(f32[32,2,2,128]{3,2,1,0:T(2,128)} %get-tuple-element.38), channel_id=1, source_target_pairs={{0,96},{32,128},{64,160},{96,192},{128,224},{160,256},{192,288},{2... | collective-permute-start | bytes 196616 | tf_op jit(solution)/shard_map/ppermute | solution.py:19
  35.7 0.9 broadcast_select_fusion.7
  36.6 10.4 %collective-permute-done.5 = f32[32,2,2,128]{3,2,1,0:T(2,128)} collective-permute-done((f32[32,2,2,128]{3,2,1,0:T(2,128)}, f32[32,2,2,128]{3,2,1,0:T(2,128)}, u32[]{:S(2)}, u32[]{:S(2)}) %collective-permute-start.5) | collective-permute-done | bytes 65568 | tf_op jit(solution)/shard_map/ppermute | solution.py:19
  47.0 0.9 broadcast_select_fusion.3
  47.9 2.9 broadcast_multiply_fusion
  50.8 4.1 %collective-permute-start.9 = (f32[32,2,2,128]{3,2,1,0:T(2,128)S(1)}, f32[32,2,2,128]{3,2,1,0:T(2,128)S(1)}, u32[]{:S(2)}, u32[]{:S(2)}) collective-permute-start(f32[32,2,2,128]{3,2,1,0:T(2,128)S(1)} %get-tuple-element.35), channel_id=1, source_target_pairs={{0,32},{32,64},{64,96},{96,128},{128,160},{160,192},{192,224},{224... | collective-permute-start | bytes 196616 | tf_op jit(solution)/shard_map/ppermute | solution.py:19
  54.9 6.9 %collective-permute-start.8 = (f32[32,2,2,128]{3,2,1,0:T(2,128)S(1)}, f32[32,2,2,128]{3,2,1,0:T(2,128)S(1)}, u32[]{:S(2)}, u32[]{:S(2)}) collective-permute-start(f32[32,2,2,128]{3,2,1,0:T(2,128)S(1)} %get-tuple-element.35), channel_id=1, source_target_pairs={{0,416},{32,448},{64,480},{96,0},{128,32},{160,64},{192,96},{224,1... | collective-permute-start | bytes 196616 | tf_op jit(solution)/shard_map/ppermute | solution.py:19
  61.9 3.1 collective-permute-start.7
  65.0 3.7 %collective-permute-start.6 = (f32[32,2,16,128]{3,2,1,0:T(8,128)S(1)}, f32[32,2,16,128]{3,2,1,0:T(8,128)S(1)}, u32[]{:S(2)}, u32[]{:S(2)}) collective-permute-start(f32[32,2,16,128]{3,2,1,0:T(8,128)S(1)} %get-tuple-element.5), channel_id=1, source_target_pairs={{0,128},{32,160},{64,192},{96,224},{128,256},{160,288},{192,320},{... | collective-permute-start | bytes 1572872 | tf_op jit(solution)/shard_map/ppermute | solution.py:19
  69.5 4.0 %collective-permute-start.11 = (f32[32,2,2,128]{3,2,1,0:T(2,128)S(1)}, f32[32,2,2,128]{3,2,1,0:T(2,128)S(1)}, u32[]{:S(2)}, u32[]{:S(2)}) collective-permute-start(f32[32,2,2,128]{3,2,1,0:T(2,128)S(1)} %get-tuple-element.36), channel_id=1, source_target_pairs={{0,480},{32,0},{64,32},{96,64},{128,96},{160,128},{192,160},{224,1... | collective-permute-start | bytes 196616 | tf_op jit(solution)/shard_map/ppermute | solution.py:19
  73.6 1.9 collective-permute-start.10
  75.6 13.0 %collective-permute-done.11 = f32[32,2,2,128]{3,2,1,0:T(2,128)S(1)} collective-permute-done((f32[32,2,2,128]{3,2,1,0:T(2,128)S(1)}, f32[32,2,2,128]{3,2,1,0:T(2,128)S(1)}, u32[]{:S(2)}, u32[]{:S(2)}) %collective-permute-start.11) | collective-permute-done | bytes 65568 | tf_op jit(solution)/shard_map/ppermute | solution.py:19
  88.6 1.1 collective-permute-done.7
  89.8 1.1 fusion.34
  90.9 1.9 collective-permute-start.15
  92.8 4.1 %collective-permute-start.14 = (f32[32,2,2,128]{3,2,1,0:T(2,128)S(1)}, f32[32,2,2,128]{3,2,1,0:T(2,128)S(1)}, u32[]{:S(2)}, u32[]{:S(2)}) collective-permute-start(f32[32,2,2,128]{3,2,1,0:T(2,128)S(1)} %get-tuple-element.25), channel_id=1, source_target_pairs={{0,416},{32,448},{64,480},{96,0},{128,32},{160,64},{192,96},{224,1... | collective-permute-start | bytes 196616 | tf_op jit(solution)/shard_map/ppermute | solution.py:19
  96.9 4.4 %collective-permute-start.13 = (f32[32,2,16,128]{3,2,1,0:T(8,128)S(1)}, f32[32,2,16,128]{3,2,1,0:T(8,128)S(1)}, u32[]{:S(2)}, u32[]{:S(2)}) collective-permute-start(f32[32,2,16,128]{3,2,1,0:T(8,128)S(1)} %fusion.34), channel_id=1, source_target_pairs={{0,384},{32,416},{64,448},{96,480},{128,0},{160,32},{192,64},{224,... | collective-permute-start | bytes 1572872 | tf_op jit(solution)/shard_map/ppermute | solution.py:19
  101.3 2.4 collective-permute-start.12
  104.0 0.2 fusion.90
  104.4 0.2 fusion.92
  104.6 4.9 %collective-permute-start.17 = (f32[32,2,2,128]{3,2,1,0:T(2,128)S(1)}, f32[32,2,2,128]{3,2,1,0:T(2,128)S(1)}, u32[]{:S(2)}, u32[]{:S(2)}) collective-permute-start(f32[32,2,2,128]{3,2,1,0:T(2,128)S(1)} %get-tuple-element.26), channel_id=1, source_target_pairs={{0,480},{32,0},{64,32},{96,64},{128,96},{160,128},{192,160},{224,1... | collective-permute-start | bytes 196616 | tf_op jit(solution)/shard_map/ppermute | solution.py:19
  109.5 2.6 collective-permute-start.16
  112.2 14.9 %collective-permute-done.17 = f32[32,2,2,128]{3,2,1,0:T(2,128)S(1)} collective-permute-done((f32[32,2,2,128]{3,2,1,0:T(2,128)S(1)}, f32[32,2,2,128]{3,2,1,0:T(2,128)S(1)}, u32[]{:S(2)}, u32[]{:S(2)}) %collective-permute-start.17) | collective-permute-done | bytes 65568 | tf_op jit(solution)/shard_map/ppermute | solution.py:19
  127.2 1.0 fusion.22
  128.3 2.9 collective-permute-start.21
  131.2 6.1 %collective-permute-start.20 = (f32[32,2,2,128]{3,2,1,0:T(2,128)S(1)}, f32[32,2,2,128]{3,2,1,0:T(2,128)S(1)}, u32[]{:S(2)}, u32[]{:S(2)}) collective-permute-start(f32[32,2,2,128]{3,2,1,0:T(2,128)S(1)} %get-tuple-element.7), channel_id=1, source_target_pairs={{0,416},{32,448},{64,480},{96,0},{128,32},{160,64},{192,96},{224,1... | collective-permute-start | bytes 196616 | tf_op jit(solution)/shard_map/ppermute | solution.py:19
  137.4 3.1 collective-permute-start.19
  140.5 3.7 %collective-permute-start.18 = (f32[32,2,16,128]{3,2,1,0:T(8,128)S(1)}, f32[32,2,16,128]{3,2,1,0:T(8,128)S(1)}, u32[]{:S(2)}, u32[]{:S(2)}) collective-permute-start(f32[32,2,16,128]{3,2,1,0:T(8,128)S(1)} %fusion.22), channel_id=1, source_target_pairs={{0,128},{32,160},{64,192},{96,224},{128,256},{160,288},{192,320},{... | collective-permute-start | bytes 1572872 | tf_op jit(solution)/shard_map/ppermute | solution.py:19
  144.6 0.2 fusion.86
  144.8 0.2 fusion.87
  145.0 4.0 %collective-permute-start.23 = (f32[32,2,2,128]{3,2,1,0:T(2,128)S(1)}, f32[32,2,2,128]{3,2,1,0:T(2,128)S(1)}, u32[]{:S(2)}, u32[]{:S(2)}) collective-permute-start(f32[32,2,2,128]{3,2,1,0:T(2,128)S(1)} %get-tuple-element.8), channel_id=1, source_target_pairs={{0,480},{32,0},{64,32},{96,64},{128,96},{160,128},{192,160},{224,1... | collective-permute-start | bytes 196616 | tf_op jit(solution)/shard_map/ppermute | solution.py:19
  149.1 1.9 collective-permute-start.22
  151.1 14.7 %collective-permute-done.23 = f32[32,2,2,128]{3,2,1,0:T(2,128)S(1)} collective-permute-done((f32[32,2,2,128]{3,2,1,0:T(2,128)S(1)}, f32[32,2,2,128]{3,2,1,0:T(2,128)S(1)}, u32[]{:S(2)}, u32[]{:S(2)}) %collective-permute-start.23) | collective-permute-done | bytes 65568 | tf_op jit(solution)/shard_map/ppermute | solution.py:19
  165.9 1.0 fusion.82
  166.9 0.8 copy.8
  167.8 139.5 %all-gather.2.cloned.1.call-done = bf16[1024,4096]{1,0:T(8,128)(2,1)} async-done(((bf16[32,4096]{1,0:T(8,128)(2,1)}), bf16[1024,4096]{1,0:T(8,128)(2,1)}) %all-gather.2.cloned.1.call-update) | async-done | bytes 8388624 | tf_op jit(solution)/shard_map/all_gather | solution.py:92
  307.2 4.9 %convolution_bitcast_fusion = f32[4,8,32,128]{3,1,2,0:T(8,128)S(1)} fusion(bf16[1024,32]{0,1:T(8,128)(2,1)S(1)} %copy-done, bf16[1024,4096]{1,0:T(8,128)(2,1)} %all-gather.2.cloned.1.call-done), kind=kOutput, calls=%fused_computation | convolution fusion | flops 268435456 | bytes 8978432 | tf_op jit(solution)/shard_map/dot_general | solution.py:90
  312.2 0.9 copy.6
  (46 shorter events, 2.3 us)
Async XLA Ops:
  6.5 300.7 %copy-start = (bf16[1024,32]{0,1:T(8,128)(2,1)S(1)}, bf16[1024,32]{0,1:T(8,128)(2,1)}, u32[]{:S(2)}) copy-start(bf16[1024,32]{0,1:T(8,128)(2,1)} %param.5) | copy-start | bytes 196612
  6.5 41.4 %copy-start.1 = (bf16[32,1,2,16,128]{4,3,2,1,0:T(8,128)(2,1)S(1)}, bf16[32,1,2,16,128]{4,3,2,1,0:T(8,128)(2,1)}, u32[]{:S(2)}) copy-start(bf16[32,1,2,16,128]{4,3,2,1,0:T(8,128)(2,1)} %param.3) | copy-start | bytes 786436
  6.5 24.7 %copy-start.2 = (f32[1,2,16,128]{3,2,1,0:T(8,128)S(1)}, f32[1,2,16,128]{3,2,1,0:T(8,128)}, u32[]{:S(2)}) copy-start(f32[1,2,16,128]{3,2,1,0:T(8,128)} %param.4) | copy-start | bytes 49156
  6.5 300.7 %all-gather.2.cloned.1.call-start = ((), (), s32[]{:S(2)}) async-start(), calls=%async_computation | async-start | bytes 8650752 | tf_op jit(solution)/shard_map/all_gather | solution.py:92
  8.3 22.9 %collective-permute-start.3 = (f32[32,2,2,128]{3,2,1,0:T(2,128)}, f32[32,2,2,128]{3,2,1,0:T(2,128)}, u32[]{:S(2)}, u32[]{:S(2)}) collective-permute-start(f32[32,2,2,128]{3,2,1,0:T(2,128)} %get-tuple-element.37), channel_id=1, source_target_pairs={{0,32},{32,64},{64,96},{96,128},{128,160},{160,192},{192,224},{224... | collective-permute-start | bytes 196616 | tf_op jit(solution)/shard_map/ppermute | solution.py:19
  12.8 22.8 %collective-permute-start.2 = (f32[32,2,2,128]{3,2,1,0:T(2,128)}, f32[32,2,2,128]{3,2,1,0:T(2,128)}, u32[]{:S(2)}, u32[]{:S(2)}) collective-permute-start(f32[32,2,2,128]{3,2,1,0:T(2,128)} %get-tuple-element.37), channel_id=1, source_target_pairs={{0,416},{32,448},{64,480},{96,0},{128,32},{160,64},{192,96},{224,1... | collective-permute-start | bytes 196616 | tf_op jit(solution)/shard_map/ppermute | solution.py:19
  17.8 30.1 %collective-permute-start.1 = (f32[32,2,16,128]{3,2,1,0:T(8,128)S(1)}, f32[32,2,16,128]{3,2,1,0:T(8,128)}, u32[]{:S(2)}, u32[]{:S(2)}) collective-permute-start(f32[32,2,16,128]{3,2,1,0:T(8,128)S(1)} %bitcast_convert_fusion), channel_id=1, source_target_pairs={{0,384},{32,416},{64,448},{96,480},{128,0},{160,32},{192,64},{224,... | collective-permute-start | bytes 1572872 | tf_op jit(solution)/shard_map/ppermute | solution.py:19
  20.9 27.0 %collective-permute-start = (f32[32,2,16,128]{3,2,1,0:T(8,128)S(1)}, f32[32,2,16,128]{3,2,1,0:T(8,128)}, u32[]{:S(2)}, u32[]{:S(2)}) collective-permute-start(f32[32,2,16,128]{3,2,1,0:T(8,128)S(1)} %bitcast_convert_fusion), channel_id=1, source_target_pairs={{0,128},{32,160},{64,192},{96,224},{128,256},{160,288},{192,320},{... | collective-permute-start | bytes 1572872 | tf_op jit(solution)/shard_map/ppermute | solution.py:19
  24.6 22.4 %collective-permute-start.5 = (f32[32,2,2,128]{3,2,1,0:T(2,128)}, f32[32,2,2,128]{3,2,1,0:T(2,128)}, u32[]{:S(2)}, u32[]{:S(2)}) collective-permute-start(f32[32,2,2,128]{3,2,1,0:T(2,128)} %get-tuple-element.38), channel_id=1, source_target_pairs={{0,480},{32,0},{64,32},{96,64},{128,96},{160,128},{192,160},{224,1... | collective-permute-start | bytes 196616 | tf_op jit(solution)/shard_map/ppermute | solution.py:19
  31.3 15.7 %collective-permute-start.4 = (f32[32,2,2,128]{3,2,1,0:T(2,128)}, f32[32,2,2,128]{3,2,1,0:T(2,128)S(1)}, u32[]{:S(2)}, u32[]{:S(2)}) collective-permute-start(f32[32,2,2,128]{3,2,1,0:T(2,128)} %get-tuple-element.38), channel_id=1, source_target_pairs={{0,96},{32,128},{64,160},{96,192},{128,224},{160,256},{192,288},{2... | collective-permute-start | bytes 196616 | tf_op jit(solution)/shard_map/ppermute | solution.py:19
  50.8 22.7 %collective-permute-start.9 = (f32[32,2,2,128]{3,2,1,0:T(2,128)S(1)}, f32[32,2,2,128]{3,2,1,0:T(2,128)S(1)}, u32[]{:S(2)}, u32[]{:S(2)}) collective-permute-start(f32[32,2,2,128]{3,2,1,0:T(2,128)S(1)} %get-tuple-element.35), channel_id=1, source_target_pairs={{0,32},{32,64},{64,96},{96,128},{128,160},{160,192},{192,224},{224... | collective-permute-start | bytes 196616 | tf_op jit(solution)/shard_map/ppermute | solution.py:19
  54.9 20.6 %collective-permute-start.8 = (f32[32,2,2,128]{3,2,1,0:T(2,128)S(1)}, f32[32,2,2,128]{3,2,1,0:T(2,128)S(1)}, u32[]{:S(2)}, u32[]{:S(2)}) collective-permute-start(f32[32,2,2,128]{3,2,1,0:T(2,128)S(1)} %get-tuple-element.35), channel_id=1, source_target_pairs={{0,416},{32,448},{64,480},{96,0},{128,32},{160,64},{192,96},{224,1... | collective-permute-start | bytes 196616 | tf_op jit(solution)/shard_map/ppermute | solution.py:19
  61.9 27.9 %collective-permute-start.7 = (f32[32,2,16,128]{3,2,1,0:T(8,128)S(1)}, f32[32,2,16,128]{3,2,1,0:T(8,128)S(1)}, u32[]{:S(2)}, u32[]{:S(2)}) collective-permute-start(f32[32,2,16,128]{3,2,1,0:T(8,128)S(1)} %get-tuple-element.5), channel_id=1, source_target_pairs={{0,384},{32,416},{64,448},{96,480},{128,0},{160,32},{192,64},{224,... | collective-permute-start | bytes 1572872 | tf_op jit(solution)/shard_map/ppermute | solution.py:19
  65.0 24.8 %collective-permute-start.6 = (f32[32,2,16,128]{3,2,1,0:T(8,128)S(1)}, f32[32,2,16,128]{3,2,1,0:T(8,128)S(1)}, u32[]{:S(2)}, u32[]{:S(2)}) collective-permute-start(f32[32,2,16,128]{3,2,1,0:T(8,128)S(1)} %get-tuple-element.5), channel_id=1, source_target_pairs={{0,128},{32,160},{64,192},{96,224},{128,256},{160,288},{192,320},{... | collective-permute-start | bytes 1572872 | tf_op jit(solution)/shard_map/ppermute | solution.py:19
  69.5 19.1 %collective-permute-start.11 = (f32[32,2,2,128]{3,2,1,0:T(2,128)S(1)}, f32[32,2,2,128]{3,2,1,0:T(2,128)S(1)}, u32[]{:S(2)}, u32[]{:S(2)}) collective-permute-start(f32[32,2,2,128]{3,2,1,0:T(2,128)S(1)} %get-tuple-element.36), channel_id=1, source_target_pairs={{0,480},{32,0},{64,32},{96,64},{128,96},{160,128},{192,160},{224,1... | collective-permute-start | bytes 196616 | tf_op jit(solution)/shard_map/ppermute | solution.py:19
  73.6 15.0 %collective-permute-start.10 = (f32[32,2,2,128]{3,2,1,0:T(2,128)S(1)}, f32[32,2,2,128]{3,2,1,0:T(2,128)S(1)}, u32[]{:S(2)}, u32[]{:S(2)}) collective-permute-start(f32[32,2,2,128]{3,2,1,0:T(2,128)S(1)} %get-tuple-element.36), channel_id=1, source_target_pairs={{0,96},{32,128},{64,160},{96,192},{128,224},{160,256},{192,288},{2... | collective-permute-start | bytes 196616 | tf_op jit(solution)/shard_map/ppermute | solution.py:19
  90.9 18.6 %collective-permute-start.15 = (f32[32,2,2,128]{3,2,1,0:T(2,128)S(1)}, f32[32,2,2,128]{3,2,1,0:T(2,128)S(1)}, u32[]{:S(2)}, u32[]{:S(2)}) collective-permute-start(f32[32,2,2,128]{3,2,1,0:T(2,128)S(1)} %get-tuple-element.25), channel_id=1, source_target_pairs={{0,32},{32,64},{64,96},{96,128},{128,160},{160,192},{192,224},{224... | collective-permute-start | bytes 196616 | tf_op jit(solution)/shard_map/ppermute | solution.py:19
  92.8 19.3 %collective-permute-start.14 = (f32[32,2,2,128]{3,2,1,0:T(2,128)S(1)}, f32[32,2,2,128]{3,2,1,0:T(2,128)S(1)}, u32[]{:S(2)}, u32[]{:S(2)}) collective-permute-start(f32[32,2,2,128]{3,2,1,0:T(2,128)S(1)} %get-tuple-element.25), channel_id=1, source_target_pairs={{0,416},{32,448},{64,480},{96,0},{128,32},{160,64},{192,96},{224,1... | collective-permute-start | bytes 196616 | tf_op jit(solution)/shard_map/ppermute | solution.py:19
  96.9 30.2 %collective-permute-start.13 = (f32[32,2,16,128]{3,2,1,0:T(8,128)S(1)}, f32[32,2,16,128]{3,2,1,0:T(8,128)S(1)}, u32[]{:S(2)}, u32[]{:S(2)}) collective-permute-start(f32[32,2,16,128]{3,2,1,0:T(8,128)S(1)} %fusion.34), channel_id=1, source_target_pairs={{0,384},{32,416},{64,448},{96,480},{128,0},{160,32},{192,64},{224,... | collective-permute-start | bytes 1572872 | tf_op jit(solution)/shard_map/ppermute | solution.py:19
  101.3 25.9 %collective-permute-start.12 = (f32[32,2,16,128]{3,2,1,0:T(8,128)S(1)}, f32[32,2,16,128]{3,2,1,0:T(8,128)S(1)}, u32[]{:S(2)}, u32[]{:S(2)}) collective-permute-start(f32[32,2,16,128]{3,2,1,0:T(8,128)S(1)} %fusion.34), channel_id=1, source_target_pairs={{0,128},{32,160},{64,192},{96,224},{128,256},{160,288},{192,320},{... | collective-permute-start | bytes 1572872 | tf_op jit(solution)/shard_map/ppermute | solution.py:19
  104.6 22.6 %collective-permute-start.17 = (f32[32,2,2,128]{3,2,1,0:T(2,128)S(1)}, f32[32,2,2,128]{3,2,1,0:T(2,128)S(1)}, u32[]{:S(2)}, u32[]{:S(2)}) collective-permute-start(f32[32,2,2,128]{3,2,1,0:T(2,128)S(1)} %get-tuple-element.26), channel_id=1, source_target_pairs={{0,480},{32,0},{64,32},{96,64},{128,96},{160,128},{192,160},{224,1... | collective-permute-start | bytes 196616 | tf_op jit(solution)/shard_map/ppermute | solution.py:19
  109.5 17.6 %collective-permute-start.16 = (f32[32,2,2,128]{3,2,1,0:T(2,128)S(1)}, f32[32,2,2,128]{3,2,1,0:T(2,128)S(1)}, u32[]{:S(2)}, u32[]{:S(2)}) collective-permute-start(f32[32,2,2,128]{3,2,1,0:T(2,128)S(1)} %get-tuple-element.26), channel_id=1, source_target_pairs={{0,96},{32,128},{64,160},{96,192},{128,224},{160,256},{192,288},{2... | collective-permute-start | bytes 196616 | tf_op jit(solution)/shard_map/ppermute | solution.py:19
  128.3 20.8 %collective-permute-start.21 = (f32[32,2,2,128]{3,2,1,0:T(2,128)S(1)}, f32[32,2,2,128]{3,2,1,0:T(2,128)S(1)}, u32[]{:S(2)}, u32[]{:S(2)}) collective-permute-start(f32[32,2,2,128]{3,2,1,0:T(2,128)S(1)} %get-tuple-element.7), channel_id=1, source_target_pairs={{0,32},{32,64},{64,96},{96,128},{128,160},{160,192},{192,224},{224... | collective-permute-start | bytes 196616 | tf_op jit(solution)/shard_map/ppermute | solution.py:19
  131.2 19.8 %collective-permute-start.20 = (f32[32,2,2,128]{3,2,1,0:T(2,128)S(1)}, f32[32,2,2,128]{3,2,1,0:T(2,128)S(1)}, u32[]{:S(2)}, u32[]{:S(2)}) collective-permute-start(f32[32,2,2,128]{3,2,1,0:T(2,128)S(1)} %get-tuple-element.7), channel_id=1, source_target_pairs={{0,416},{32,448},{64,480},{96,0},{128,32},{160,64},{192,96},{224,1... | collective-permute-start | bytes 196616 | tf_op jit(solution)/shard_map/ppermute | solution.py:19
  137.4 28.5 %collective-permute-start.19 = (f32[32,2,16,128]{3,2,1,0:T(8,128)S(1)}, f32[32,2,16,128]{3,2,1,0:T(8,128)S(1)}, u32[]{:S(2)}, u32[]{:S(2)}) collective-permute-start(f32[32,2,16,128]{3,2,1,0:T(8,128)S(1)} %fusion.22), channel_id=1, source_target_pairs={{0,384},{32,416},{64,448},{96,480},{128,0},{160,32},{192,64},{224,... | collective-permute-start | bytes 1572872 | tf_op jit(solution)/shard_map/ppermute | solution.py:19
  140.5 25.4 %collective-permute-start.18 = (f32[32,2,16,128]{3,2,1,0:T(8,128)S(1)}, f32[32,2,16,128]{3,2,1,0:T(8,128)S(1)}, u32[]{:S(2)}, u32[]{:S(2)}) collective-permute-start(f32[32,2,16,128]{3,2,1,0:T(8,128)S(1)} %fusion.22), channel_id=1, source_target_pairs={{0,128},{32,160},{64,192},{96,224},{128,256},{160,288},{192,320},{... | collective-permute-start | bytes 1572872 | tf_op jit(solution)/shard_map/ppermute | solution.py:19
  145.0 20.8 %collective-permute-start.23 = (f32[32,2,2,128]{3,2,1,0:T(2,128)S(1)}, f32[32,2,2,128]{3,2,1,0:T(2,128)S(1)}, u32[]{:S(2)}, u32[]{:S(2)}) collective-permute-start(f32[32,2,2,128]{3,2,1,0:T(2,128)S(1)} %get-tuple-element.8), channel_id=1, source_target_pairs={{0,480},{32,0},{64,32},{96,64},{128,96},{160,128},{192,160},{224,1... | collective-permute-start | bytes 196616 | tf_op jit(solution)/shard_map/ppermute | solution.py:19
  149.1 16.7 %collective-permute-start.22 = (f32[32,2,2,128]{3,2,1,0:T(2,128)S(1)}, f32[32,2,2,128]{3,2,1,0:T(2,128)S(1)}, u32[]{:S(2)}, u32[]{:S(2)}) collective-permute-start(f32[32,2,2,128]{3,2,1,0:T(2,128)S(1)} %get-tuple-element.8), channel_id=1, source_target_pairs={{0,96},{32,128},{64,160},{96,192},{128,224},{160,256},{192,288},{2... | collective-permute-start | bytes 196616 | tf_op jit(solution)/shard_map/ppermute | solution.py:19
Sparse Core Ops, SparseCore 0:
  167.9 139.3 all-gather.1
where the time goes:
time: 321 us; the launch traced here: 320 us
  waiting for transfers between devices  194 us (60%)
  starting transfers between devices  90.6 us (28%)
  between operations  13.8 us (4%)
  other arithmetic  9.05 us (3%)
  local copies, waits for them, and re-layouts  7.66 us (2%)
  matrix products  4.92 us (2%)
    all_gather x1, waiting for transfers between devices, on_device(): lax.all_gather(flat_panel, 'band', axis=0, tiled=True)  139 us
    ppermute x24, starting transfers between devices, shifted(): return lax.ppermute(value, axis, pairs)  90.6 us
    ppermute x24, waiting for transfers between devices, shifted(): return lax.ppermute(value, axis, pairs)  54.3 us
  transfers between devices with their start and end apart: 25, of which 6 were waited for; matrix products, arithmetic and copies ran while one was open for 2% of the time, Pallas kernels for 0%

commit v1 on v0

--- a/solution.py
+++ b/solution.py
@@ -89,7 +89,9 @@
     flat_panel = current.astype(jnp.bfloat16).reshape(band_rows, -1)
     rotated = lax.dot_general(
         ritz,
-        lax.all_gather(flat_panel, "band", axis=0, tiled=True),
+        jnp.concatenate(
+            lax.all_to_all(jnp.stack([flat_panel] * lax.axis_size("band")), "band", 0, 0), axis=0
+        ),
         (((0,), (0,)), ((), ())),
         preferred_element_type=jnp.float32,
     )

time: 321 us -> 386 us (1.20)
  the two profiles are of different devices: /device:TPU:1 before, /device:TPU:91 now
where the time goes in v1:
time: 386 us; the launch traced here: 385 us
  blocking collectives  227 us (59%)
  starting transfers between devices  84.1 us (22%)
  waiting for transfers between devices  55.5 us (14%)
  other arithmetic  8.23 us (2%)
  local copies, waits for them, and re-layouts  7.99 us (2%)
    all_to_all x1, blocking collectives, on_device(): lax.all_to_all(jnp.stack([flat_panel] * lax.axis_size('band')), 'band', 0...  227 us
    ppermute x24, starting transfers between devices, shifted(): return lax.ppermute(value, axis, pairs)  84.1 us
    ppermute x24, waiting for transfers between devices, shifted(): return lax.ppermute(value, axis, pairs)  55.5 us
  transfers between devices with their start and end apart: 24, of which 8 were waited for; matrix products, arithmetic and copies ran while one was open for 2% of the time, Pallas kernels for 0%

profile of v1, /device:TPU:91, one launch (start us, length us, event | category | flops | bytes accessed | tf_op | source)
XLA Modules:
  0.0 384.9 jit_solution(3895674172984278480)
XLA Ops:
  0.0 1.1 bitcast_convert_fusion
  1.1 0.7 fusion.99
  1.8 3.7 collective-permute-start.3
  5.5 1.9 collective-permute-start.2
  7.4 3.6 collective-permute-start.1
  11.0 3.1 collective-permute-start
  14.2 4.6 %collective-permute-start.5 = (f32[32,2,2,128]{3,2,1,0:T(2,128)}, f32[32,2,2,128]{3,2,1,0:T(2,128)}, u32[]{:S(2)}, u32[]{:S(2)}) collective-permute-start(f32[32,2,2,128]{3,2,1,0:T(2,128)} %get-tuple-element.38), channel_id=1, source_target_pairs={{0,480},{32,0},{64,32},{96,64},{128,96},{160,128},{192,160},{224,1... | collective-permute-start | bytes 196616 | tf_op jit(solution)/shard_map/ppermute | solution.py:19
  19.0 0.2 fusion.100
  19.2 1.0 fusion.103
  20.2 1.1 fusion.102
  21.4 3.9 %collective-permute-start.4 = (f32[32,2,2,128]{3,2,1,0:T(2,128)}, f32[32,2,2,128]{3,2,1,0:T(2,128)S(1)}, u32[]{:S(2)}, u32[]{:S(2)}) collective-permute-start(f32[32,2,2,128]{3,2,1,0:T(2,128)} %get-tuple-element.38), channel_id=1, source_target_pairs={{0,96},{32,128},{64,160},{96,192},{128,224},{160,256},{192,288},{2... | collective-permute-start | bytes 196616 | tf_op jit(solution)/shard_map/ppermute | solution.py:19
  25.3 0.9 broadcast_select_fusion.7
  26.2 10.9 %collective-permute-done.5 = f32[32,2,2,128]{3,2,1,0:T(2,128)} collective-permute-done((f32[32,2,2,128]{3,2,1,0:T(2,128)}, f32[32,2,2,128]{3,2,1,0:T(2,128)}, u32[]{:S(2)}, u32[]{:S(2)}) %collective-permute-start.5) | collective-permute-done | bytes 65568 | tf_op jit(solution)/shard_map/ppermute | solution.py:19
  37.2 0.6 collective-permute-done.4
  37.8 2.9 broadcast_multiply_fusion
  40.7 4.4 %collective-permute-start.9 = (f32[32,2,2,128]{3,2,1,0:T(2,128)S(1)}, f32[32,2,2,128]{3,2,1,0:T(2,128)S(1)}, u32[]{:S(2)}, u32[]{:S(2)}) collective-permute-start(f32[32,2,2,128]{3,2,1,0:T(2,128)S(1)} %get-tuple-element.35), channel_id=1, source_target_pairs={{0,32},{32,64},{64,96},{96,128},{128,160},{160,192},{192,224},{224... | collective-permute-start | bytes 196616 | tf_op jit(solution)/shard_map/ppermute | solution.py:19
  45.1 1.9 collective-permute-start.8
  47.1 2.9 collective-permute-start.7
  50.0 3.9 %collective-permute-start.6 = (f32[32,2,16,128]{3,2,1,0:T(8,128)S(1)}, f32[32,2,16,128]{3,2,1,0:T(8,128)S(1)}, u32[]{:S(2)}, u32[]{:S(2)}) collective-permute-start(f32[32,2,16,128]{3,2,1,0:T(8,128)S(1)} %get-tuple-element.5), channel_id=1, source_target_pairs={{0,128},{32,160},{64,192},{96,224},{128,256},{160,288},{192,320},{... | collective-permute-start | bytes 1572872 | tf_op jit(solution)/shard_map/ppermute | solution.py:19
  54.7 3.8 collective-permute-start.11
  58.6 4.7 %collective-permute-start.10 = (f32[32,2,2,128]{3,2,1,0:T(2,128)S(1)}, f32[32,2,2,128]{3,2,1,0:T(2,128)S(1)}, u32[]{:S(2)}, u32[]{:S(2)}) collective-permute-start(f32[32,2,2,128]{3,2,1,0:T(2,128)S(1)} %get-tuple-element.36), channel_id=1, source_target_pairs={{0,96},{32,128},{64,160},{96,192},{128,224},{160,256},{192,288},{2... | collective-permute-start | bytes 196616 | tf_op jit(solution)/shard_map/ppermute | solution.py:19
  63.3 13.4 %collective-permute-done.11 = f32[32,2,2,128]{3,2,1,0:T(2,128)S(1)} collective-permute-done((f32[32,2,2,128]{3,2,1,0:T(2,128)S(1)}, f32[32,2,2,128]{3,2,1,0:T(2,128)S(1)}, u32[]{:S(2)}, u32[]{:S(2)}) %collective-permute-start.11) | collective-permute-done | bytes 65568 | tf_op jit(solution)/shard_map/ppermute | solution.py:19
  76.8 0.9 collective-permute-done.10
  77.7 1.1 fusion.34
  78.9 3.6 collective-permute-start.15
  82.4 2.2 collective-permute-start.14
  84.6 4.6 %collective-permute-start.13 = (f32[32,2,16,128]{3,2,1,0:T(8,128)S(1)}, f32[32,2,16,128]{3,2,1,0:T(8,128)S(1)}, u32[]{:S(2)}, u32[]{:S(2)}) collective-permute-start(f32[32,2,16,128]{3,2,1,0:T(8,128)S(1)} %fusion.34), channel_id=1, source_target_pairs={{0,384},{32,416},{64,448},{96,480},{128,0},{160,32},{192,64},{224,... | collective-permute-start | bytes 1572872 | tf_op jit(solution)/shard_map/ppermute | solution.py:19
  89.2 2.2 collective-permute-start.12
  92.1 0.2 fusion.92
  92.3 5.5 %collective-permute-start.17 = (f32[32,2,2,128]{3,2,1,0:T(2,128)S(1)}, f32[32,2,2,128]{3,2,1,0:T(2,128)S(1)}, u32[]{:S(2)}, u32[]{:S(2)}) collective-permute-start(f32[32,2,2,128]{3,2,1,0:T(2,128)S(1)} %get-tuple-element.26), channel_id=1, source_target_pairs={{0,480},{32,0},{64,32},{96,64},{128,96},{160,128},{192,160},{224,1... | collective-permute-start | bytes 196616 | tf_op jit(solution)/shard_map/ppermute | solution.py:19
  97.8 2.7 collective-permute-start.16
  100.6 13.7 %collective-permute-done.17 = f32[32,2,2,128]{3,2,1,0:T(2,128)S(1)} collective-permute-done((f32[32,2,2,128]{3,2,1,0:T(2,128)S(1)}, f32[32,2,2,128]{3,2,1,0:T(2,128)S(1)}, u32[]{:S(2)}, u32[]{:S(2)}) %collective-permute-start.17) | collective-permute-done | bytes 65568 | tf_op jit(solution)/shard_map/ppermute | solution.py:19
  114.3 0.9 collective-permute-done.16
  115.2 1.0 fusion.22
  116.3 3.6 collective-permute-start.21
  119.9 1.9 collective-permute-start.20
  121.9 3.7 collective-permute-start.19
  125.6 3.1 collective-permute-start.18
  128.9 0.2 fusion.85
  129.5 4.7 %collective-permute-start.23 = (f32[32,2,2,128]{3,2,1,0:T(2,128)S(1)}, f32[32,2,2,128]{3,2,1,0:T(2,128)S(1)}, u32[]{:S(2)}, u32[]{:S(2)}) collective-permute-start(f32[32,2,2,128]{3,2,1,0:T(2,128)S(1)} %get-tuple-element.8), channel_id=1, source_target_pairs={{0,480},{32,0},{64,32},{96,64},{128,96},{160,128},{192,160},{224,1... | collective-permute-start | bytes 196616 | tf_op jit(solution)/shard_map/ppermute | solution.py:19
  134.2 3.9 %collective-permute-start.22 = (f32[32,2,2,128]{3,2,1,0:T(2,128)S(1)}, f32[32,2,2,128]{3,2,1,0:T(2,128)S(1)}, u32[]{:S(2)}, u32[]{:S(2)}) collective-permute-start(f32[32,2,2,128]{3,2,1,0:T(2,128)S(1)} %get-tuple-element.8), channel_id=1, source_target_pairs={{0,96},{32,128},{64,160},{96,192},{128,224},{160,256},{192,288},{2... | collective-permute-start | bytes 196616 | tf_op jit(solution)/shard_map/ppermute | solution.py:19
  138.1 13.4 %collective-permute-done.23 = f32[32,2,2,128]{3,2,1,0:T(2,128)S(1)} collective-permute-done((f32[32,2,2,128]{3,2,1,0:T(2,128)S(1)}, f32[32,2,2,128]{3,2,1,0:T(2,128)S(1)}, u32[]{:S(2)}, u32[]{:S(2)}) %collective-permute-start.23) | collective-permute-done | bytes 65568 | tf_op jit(solution)/shard_map/ppermute | solution.py:19
  151.6 1.6 collective-permute-done.22
  153.3 1.0 fusion.82
  154.4 1.0 stack.3
  155.5 227.0 %all_to_all.5 = bf16[32,32,4096]{2,1,0:T(8,128)(2,1)S(1)} all-to-all(bf16[32,32,4096]{2,1,0:T(8,128)(2,1)S(1)} %stack.3), channel_id=1, replica_groups=mesh['dom'=16,'band'=32] {'band'}, dimensions={0} | all-to-all | bytes 16777216 | tf_op jit(solution)/shard_map/all_to_all | solution.py:93
  382.5 1.5 convolution_bitcast_fusion
  384.1 0.9 copy.6
  (45 shorter events, 2.9 us)
Async XLA Ops:
  0.0 382.5 %copy-start = (bf16[1024,32]{0,1:T(8,128)(2,1)S(1)}, bf16[1024,32]{0,1:T(8,128)(2,1)}, u32[]{:S(2)}) copy-start(bf16[1024,32]{0,1:T(8,128)(2,1)} %param.5) | copy-start | bytes 196612
  0.0 37.8 %copy-start.1 = (bf16[32,1,2,16,128]{4,3,2,1,0:T(8,128)(2,1)S(1)}, bf16[32,1,2,16,128]{4,3,2,1,0:T(8,128)(2,1)}, u32[]{:S(2)}) copy-start(bf16[32,1,2,16,128]{4,3,2,1,0:T(8,128)(2,1)} %param.3) | copy-start | bytes 786436
  0.0 21.3 %copy-start.2 = (f32[1,2,16,128]{3,2,1,0:T(8,128)S(1)}, f32[1,2,16,128]{3,2,1,0:T(8,128)}, u32[]{:S(2)}) copy-start(f32[1,2,16,128]{3,2,1,0:T(8,128)} %param.4) | copy-start | bytes 49156
  1.8 19.6 %collective-permute-start.3 = (f32[32,2,2,128]{3,2,1,0:T(2,128)}, f32[32,2,2,128]{3,2,1,0:T(2,128)}, u32[]{:S(2)}, u32[]{:S(2)}) collective-permute-start(f32[32,2,2,128]{3,2,1,0:T(2,128)} %get-tuple-element.37), channel_id=1, source_target_pairs={{0,32},{32,64},{64,96},{96,128},{128,160},{160,192},{192,224},{224... | collective-permute-start | bytes 196616 | tf_op jit(solution)/shard_map/ppermute | solution.py:19
  5.5 19.9 %collective-permute-start.2 = (f32[32,2,2,128]{3,2,1,0:T(2,128)}, f32[32,2,2,128]{3,2,1,0:T(2,128)}, u32[]{:S(2)}, u32[]{:S(2)}) collective-permute-start(f32[32,2,2,128]{3,2,1,0:T(2,128)} %get-tuple-element.37), channel_id=1, source_target_pairs={{0,416},{32,448},{64,480},{96,0},{128,32},{160,64},{192,96},{224,1... | collective-permute-start | bytes 196616 | tf_op jit(solution)/shard_map/ppermute | solution.py:19
  7.4 30.4 %collective-permute-start.1 = (f32[32,2,16,128]{3,2,1,0:T(8,128)S(1)}, f32[32,2,16,128]{3,2,1,0:T(8,128)}, u32[]{:S(2)}, u32[]{:S(2)}) collective-permute-start(f32[32,2,16,128]{3,2,1,0:T(8,128)S(1)} %bitcast_convert_fusion), channel_id=1, source_target_pairs={{0,384},{32,416},{64,448},{96,480},{128,0},{160,32},{192,64},{224,... | collective-permute-start | bytes 1572872 | tf_op jit(solution)/shard_map/ppermute | solution.py:19
  11.0 26.8 %collective-permute-start = (f32[32,2,16,128]{3,2,1,0:T(8,128)S(1)}, f32[32,2,16,128]{3,2,1,0:T(8,128)}, u32[]{:S(2)}, u32[]{:S(2)}) collective-permute-start(f32[32,2,16,128]{3,2,1,0:T(8,128)S(1)} %bitcast_convert_fusion), channel_id=1, source_target_pairs={{0,128},{32,160},{64,192},{96,224},{128,256},{160,288},{192,320},{... | collective-permute-start | bytes 1572872 | tf_op jit(solution)/shard_map/ppermute | solution.py:19
  14.2 23.0 %collective-permute-start.5 = (f32[32,2,2,128]{3,2,1,0:T(2,128)}, f32[32,2,2,128]{3,2,1,0:T(2,128)}, u32[]{:S(2)}, u32[]{:S(2)}) collective-permute-start(f32[32,2,2,128]{3,2,1,0:T(2,128)} %get-tuple-element.38), channel_id=1, source_target_pairs={{0,480},{32,0},{64,32},{96,64},{128,96},{160,128},{192,160},{224,1... | collective-permute-start | bytes 196616 | tf_op jit(solution)/shard_map/ppermute | solution.py:19
  21.4 16.4 %collective-permute-start.4 = (f32[32,2,2,128]{3,2,1,0:T(2,128)}, f32[32,2,2,128]{3,2,1,0:T(2,128)S(1)}, u32[]{:S(2)}, u32[]{:S(2)}) collective-permute-start(f32[32,2,2,128]{3,2,1,0:T(2,128)} %get-tuple-element.38), channel_id=1, source_target_pairs={{0,96},{32,128},{64,160},{96,192},{128,224},{160,256},{192,288},{2... | collective-permute-start | bytes 196616 | tf_op jit(solution)/shard_map/ppermute | solution.py:19
  40.7 17.8 %collective-permute-start.9 = (f32[32,2,2,128]{3,2,1,0:T(2,128)S(1)}, f32[32,2,2,128]{3,2,1,0:T(2,128)S(1)}, u32[]{:S(2)}, u32[]{:S(2)}) collective-permute-start(f32[32,2,2,128]{3,2,1,0:T(2,128)S(1)} %get-tuple-element.35), channel_id=1, source_target_pairs={{0,32},{32,64},{64,96},{96,128},{128,160},{160,192},{192,224},{224... | collective-permute-start | bytes 196616 | tf_op jit(solution)/shard_map/ppermute | solution.py:19
  45.1 18.1 %collective-permute-start.8 = (f32[32,2,2,128]{3,2,1,0:T(2,128)S(1)}, f32[32,2,2,128]{3,2,1,0:T(2,128)S(1)}, u32[]{:S(2)}, u32[]{:S(2)}) collective-permute-start(f32[32,2,2,128]{3,2,1,0:T(2,128)S(1)} %get-tuple-element.35), channel_id=1, source_target_pairs={{0,416},{32,448},{64,480},{96,0},{128,32},{160,64},{192,96},{224,1... | collective-permute-start | bytes 196616 | tf_op jit(solution)/shard_map/ppermute | solution.py:19
  47.1 30.6 %collective-permute-start.7 = (f32[32,2,16,128]{3,2,1,0:T(8,128)S(1)}, f32[32,2,16,128]{3,2,1,0:T(8,128)S(1)}, u32[]{:S(2)}, u32[]{:S(2)}) collective-permute-start(f32[32,2,16,128]{3,2,1,0:T(8,128)S(1)} %get-tuple-element.5), channel_id=1, source_target_pairs={{0,384},{32,416},{64,448},{96,480},{128,0},{160,32},{192,64},{224,... | collective-permute-start | bytes 1572872 | tf_op jit(solution)/shard_map/ppermute | solution.py:19
  50.0 27.8 %collective-permute-start.6 = (f32[32,2,16,128]{3,2,1,0:T(8,128)S(1)}, f32[32,2,16,128]{3,2,1,0:T(8,128)S(1)}, u32[]{:S(2)}, u32[]{:S(2)}) collective-permute-start(f32[32,2,16,128]{3,2,1,0:T(8,128)S(1)} %get-tuple-element.5), channel_id=1, source_target_pairs={{0,128},{32,160},{64,192},{96,224},{128,256},{160,288},{192,320},{... | collective-permute-start | bytes 1572872 | tf_op jit(solution)/shard_map/ppermute | solution.py:19
  54.7 22.0 %collective-permute-start.11 = (f32[32,2,2,128]{3,2,1,0:T(2,128)S(1)}, f32[32,2,2,128]{3,2,1,0:T(2,128)S(1)}, u32[]{:S(2)}, u32[]{:S(2)}) collective-permute-start(f32[32,2,2,128]{3,2,1,0:T(2,128)S(1)} %get-tuple-element.36), channel_id=1, source_target_pairs={{0,480},{32,0},{64,32},{96,64},{128,96},{160,128},{192,160},{224,1... | collective-permute-start | bytes 196616 | tf_op jit(solution)/shard_map/ppermute | solution.py:19
  58.6 19.1 %collective-permute-start.10 = (f32[32,2,2,128]{3,2,1,0:T(2,128)S(1)}, f32[32,2,2,128]{3,2,1,0:T(2,128)S(1)}, u32[]{:S(2)}, u32[]{:S(2)}) collective-permute-start(f32[32,2,2,128]{3,2,1,0:T(2,128)S(1)} %get-tuple-element.36), channel_id=1, source_target_pairs={{0,96},{32,128},{64,160},{96,192},{128,224},{160,256},{192,288},{2... | collective-permute-start | bytes 196616 | tf_op jit(solution)/shard_map/ppermute | solution.py:19
  78.9 19.0 %collective-permute-start.15 = (f32[32,2,2,128]{3,2,1,0:T(2,128)S(1)}, f32[32,2,2,128]{3,2,1,0:T(2,128)S(1)}, u32[]{:S(2)}, u32[]{:S(2)}) collective-permute-start(f32[32,2,2,128]{3,2,1,0:T(2,128)S(1)} %get-tuple-element.25), channel_id=1, source_target_pairs={{0,32},{32,64},{64,96},{96,128},{128,160},{160,192},{192,224},{224... | collective-permute-start | bytes 196616 | tf_op jit(solution)/shard_map/ppermute | solution.py:19
  82.4 18.1 %collective-permute-start.14 = (f32[32,2,2,128]{3,2,1,0:T(2,128)S(1)}, f32[32,2,2,128]{3,2,1,0:T(2,128)S(1)}, u32[]{:S(2)}, u32[]{:S(2)}) collective-permute-start(f32[32,2,2,128]{3,2,1,0:T(2,128)S(1)} %get-tuple-element.25), channel_id=1, source_target_pairs={{0,416},{32,448},{64,480},{96,0},{128,32},{160,64},{192,96},{224,1... | collective-permute-start | bytes 196616 | tf_op jit(solution)/shard_map/ppermute | solution.py:19
  84.6 30.6 %collective-permute-start.13 = (f32[32,2,16,128]{3,2,1,0:T(8,128)S(1)}, f32[32,2,16,128]{3,2,1,0:T(8,128)S(1)}, u32[]{:S(2)}, u32[]{:S(2)}) collective-permute-start(f32[32,2,16,128]{3,2,1,0:T(8,128)S(1)} %fusion.34), channel_id=1, source_target_pairs={{0,384},{32,416},{64,448},{96,480},{128,0},{160,32},{192,64},{224,... | collective-permute-start | bytes 1572872 | tf_op jit(solution)/shard_map/ppermute | solution.py:19
  89.2 26.0 %collective-permute-start.12 = (f32[32,2,16,128]{3,2,1,0:T(8,128)S(1)}, f32[32,2,16,128]{3,2,1,0:T(8,128)S(1)}, u32[]{:S(2)}, u32[]{:S(2)}) collective-permute-start(f32[32,2,16,128]{3,2,1,0:T(8,128)S(1)} %fusion.34), channel_id=1, source_target_pairs={{0,128},{32,160},{64,192},{96,224},{128,256},{160,288},{192,320},{... | collective-permute-start | bytes 1572872 | tf_op jit(solution)/shard_map/ppermute | solution.py:19
  92.3 22.0 %collective-permute-start.17 = (f32[32,2,2,128]{3,2,1,0:T(2,128)S(1)}, f32[32,2,2,128]{3,2,1,0:T(2,128)S(1)}, u32[]{:S(2)}, u32[]{:S(2)}) collective-permute-start(f32[32,2,2,128]{3,2,1,0:T(2,128)S(1)} %get-tuple-element.26), channel_id=1, source_target_pairs={{0,480},{32,0},{64,32},{96,64},{128,96},{160,128},{192,160},{224,1... | collective-permute-start | bytes 196616 | tf_op jit(solution)/shard_map/ppermute | solution.py:19
  97.8 17.4 %collective-permute-start.16 = (f32[32,2,2,128]{3,2,1,0:T(2,128)S(1)}, f32[32,2,2,128]{3,2,1,0:T(2,128)S(1)}, u32[]{:S(2)}, u32[]{:S(2)}) collective-permute-start(f32[32,2,2,128]{3,2,1,0:T(2,128)S(1)} %get-tuple-element.26), channel_id=1, source_target_pairs={{0,96},{32,128},{64,160},{96,192},{128,224},{160,256},{192,288},{2... | collective-permute-start | bytes 196616 | tf_op jit(solution)/shard_map/ppermute | solution.py:19
  116.3 17.8 %collective-permute-start.21 = (f32[32,2,2,128]{3,2,1,0:T(2,128)S(1)}, f32[32,2,2,128]{3,2,1,0:T(2,128)S(1)}, u32[]{:S(2)}, u32[]{:S(2)}) collective-permute-start(f32[32,2,2,128]{3,2,1,0:T(2,128)S(1)} %get-tuple-element.7), channel_id=1, source_target_pairs={{0,32},{32,64},{64,96},{96,128},{128,160},{160,192},{192,224},{224... | collective-permute-start | bytes 196616 | tf_op jit(solution)/shard_map/ppermute | solution.py:19
  119.9 18.1 %collective-permute-start.20 = (f32[32,2,2,128]{3,2,1,0:T(2,128)S(1)}, f32[32,2,2,128]{3,2,1,0:T(2,128)S(1)}, u32[]{:S(2)}, u32[]{:S(2)}) collective-permute-start(f32[32,2,2,128]{3,2,1,0:T(2,128)S(1)} %get-tuple-element.7), channel_id=1, source_target_pairs={{0,416},{32,448},{64,480},{96,0},{128,32},{160,64},{192,96},{224,1... | collective-permute-start | bytes 196616 | tf_op jit(solution)/shard_map/ppermute | solution.py:19
  121.9 31.4 %collective-permute-start.19 = (f32[32,2,16,128]{3,2,1,0:T(8,128)S(1)}, f32[32,2,16,128]{3,2,1,0:T(8,128)S(1)}, u32[]{:S(2)}, u32[]{:S(2)}) collective-permute-start(f32[32,2,16,128]{3,2,1,0:T(8,128)S(1)} %fusion.22), channel_id=1, source_target_pairs={{0,384},{32,416},{64,448},{96,480},{128,0},{160,32},{192,64},{224,... | collective-permute-start | bytes 1572872 | tf_op jit(solution)/shard_map/ppermute | solution.py:19
  125.6 27.7 %collective-permute-start.18 = (f32[32,2,16,128]{3,2,1,0:T(8,128)S(1)}, f32[32,2,16,128]{3,2,1,0:T(8,128)S(1)}, u32[]{:S(2)}, u32[]{:S(2)}) collective-permute-start(f32[32,2,16,128]{3,2,1,0:T(8,128)S(1)} %fusion.22), channel_id=1, source_target_pairs={{0,128},{32,160},{64,192},{96,224},{128,256},{160,288},{192,320},{... | collective-permute-start | bytes 1572872 | tf_op jit(solution)/shard_map/ppermute | solution.py:19
  129.5 22.0 %collective-permute-start.23 = (f32[32,2,2,128]{3,2,1,0:T(2,128)S(1)}, f32[32,2,2,128]{3,2,1,0:T(2,128)S(1)}, u32[]{:S(2)}, u32[]{:S(2)}) collective-permute-start(f32[32,2,2,128]{3,2,1,0:T(2,128)S(1)} %get-tuple-element.8), channel_id=1, source_target_pairs={{0,480},{32,0},{64,32},{96,64},{128,96},{160,128},{192,160},{224,1... | collective-permute-start | bytes 196616 | tf_op jit(solution)/shard_map/ppermute | solution.py:19
  134.2 19.0 %collective-permute-start.22 = (f32[32,2,2,128]{3,2,1,0:T(2,128)S(1)}, f32[32,2,2,128]{3,2,1,0:T(2,128)S(1)}, u32[]{:S(2)}, u32[]{:S(2)}) collective-permute-start(f32[32,2,2,128]{3,2,1,0:T(2,128)S(1)} %get-tuple-element.8), channel_id=1, source_target_pairs={{0,96},{32,128},{64,160},{96,192},{128,224},{160,256},{192,288},{2... | collective-permute-start | bytes 196616 | tf_op jit(solution)/shard_map/ppermute | solution.py:19
